TPU v7x, 32 devices: a whole 2x2x4 slice. The times are simulated.
32 devices in a mesh: grp: 4 (over y, x), slab: 8 (over z, core).
Axes of the slice: x: 2, y: 2, z: 4, core: 2. Of those that a mesh axis runs over, the one named last changes fastest.
Arguments:
- fields: float32 [64, 64, 8, 128], P('grp', 'slab'), may hold values from -6 to 6
- velocity: int32 [3, 64, 8, 128], P(None, 'slab'), may hold values from -2 to 2
- diffusivity: float32 [64, 8, 128], P('slab'), may hold values from 0.005 to 0.04
- sensor_offsets: int32 [49152], P('slab'), may hold values from 0 to 8191
- sensor_counts: int32 [8], P('slab'), may hold values from 1 to 6144, 16384 in all
- observations: float32 [49152], P('slab'), may hold values from -6 to 6
- noise_scale: float32 [49152], P('slab'), may hold values from 2 to 20
- perturbation: float32 [64, 49152], P('grp', 'slab'), may hold values from -6 to 6
Outputs:
- updated: float32 [64, 64, 8, 128], P('grp', 'slab')
Inputs may be any that keep to these rules, and one draw needn't show every extreme that they name: `sensor_counts`: the counts sum to 16384 and the largest is exactly 6144. `sensor_offsets`: slots at or past their slab's count are unused.
All inputs are finite; a program needn't handle non-finite values. No bound on the sum of `sensor_counts` on one device may be relied on, other than what follows from the above.
Results may differ from a plain program's by a relative error of at most 0.00011.
Values sent between devices are 32-bit elements; how exact they have to be, the bound alone decides.
A program may use at most 64 MiB of HBM per device.

v0:
```python
import math

import jax
import jax.numpy as jnp
from jax import lax
from jax.sharding import PartitionSpec as P

STEPS = 2


COURANT = 0.12


def extended_2(array, sides, width):
    for axis, dim in sides:
        size, length = (lax.axis_size(axis), array.shape[dim])
        up = [(i, (i + 1) % size) for i in range(size - 1)]
        down = [(j, i) for i, j in up]
        last = lax.slice_in_dim(array, length - width, length, axis=dim)
        initial = lax.slice_in_dim(array, 0, width, axis=dim)
        before = lax.ppermute(last, axis, up)
        after = lax.ppermute(initial, axis, down)
        array = jnp.concatenate([before, array, after], axis=dim)
    return array


def upwind(courant, center, lower_side, upper_side):
    return jnp.maximum(courant, 0.0) * (center - lower_side) + jnp.minimum(courant, 0.0) * (
        upper_side - center
    )


def advance(extended, courant, diffusivity):
    center = extended[:, 1:-1]
    below = extended[:, :-2]
    above = extended[:, 2:]
    south = jnp.roll(center, 1, axis=2)
    north = jnp.roll(center, -1, axis=2)
    west = jnp.roll(center, 1, axis=3)
    east = jnp.roll(center, -1, axis=3)
    transport = upwind(courant[0], center, below, above) + upwind(courant[1], center, south, north)
    transport = transport + upwind(courant[2], center, west, east)
    laplace = below + above + south + north + west + east - 6.0 * center
    return center - transport + diffusivity * laplace


def solve_weights(gram_matrix, cross_matrix, spread_root):
    order = gram_matrix.shape[0]
    index_row = jnp.arange(order, dtype=jnp.int32)
    system = jnp.eye(order, dtype=jnp.float32) + gram_matrix

    def factor_column(column, lower_factor):
        row_here = lax.dynamic_slice_in_dim(lower_factor, column, 1, 0)[0]
        needed = lax.dynamic_slice_in_dim(system, column, 1, 1)[:, 0]
        needed = needed - jnp.dot(
            lower_factor,
            row_here,
            precision=lax.Precision.HIGHEST,
            preferred_element_type=jnp.float32,
        )
        pivot = jnp.sqrt(lax.dynamic_slice_in_dim(needed, column, 1, 0)[0])
        values = jnp.where(index_row >= column, needed / pivot, 0.0)
        marker = (index_row == column).astype(jnp.float32)
        return lower_factor + values[:, None] * marker[None, :]

    lower_factor = lax.fori_loop(0, order, factor_column, jnp.zeros((order, order), jnp.float32))

    def forward_row(row, solved):
        factor_row = lax.dynamic_slice_in_dim(lower_factor, row, 1, 0)[0]
        pivot = lax.dynamic_slice_in_dim(factor_row, row, 1, 0)[0]
        given = lax.dynamic_slice_in_dim(cross_matrix, row, 1, 0)[0]
        value = (
            given
            - jnp.dot(
                factor_row,
                solved,
                precision=lax.Precision.HIGHEST,
                preferred_element_type=jnp.float32,
            )
        ) / pivot
        return lax.dynamic_update_slice_in_dim(solved, value[None, :], row, 0)

    middle = lax.fori_loop(0, order, forward_row, jnp.zeros_like(cross_matrix))

    def backward_row(turn, solved):
        row = order - 1 - turn
        factor_col = lax.dynamic_slice_in_dim(lower_factor, row, 1, 1)[:, 0]
        pivot = lax.dynamic_slice_in_dim(factor_col, row, 1, 0)[0]
        given = lax.dynamic_slice_in_dim(middle, row, 1, 0)[0]
        value = (
            given
            - jnp.dot(
                factor_col,
                solved,
                precision=lax.Precision.HIGHEST,
                preferred_element_type=jnp.float32,
            )
        ) / pivot
        return lax.dynamic_update_slice_in_dim(solved, value[None, :], row, 0)

    result = lax.fori_loop(0, order, backward_row, jnp.zeros_like(cross_matrix))
    return result / spread_root


def ensemble_parts(centered, misfit_rows):
    gram_part = jnp.dot(
        centered, centered.T, precision=lax.Precision.HIGHEST, preferred_element_type=jnp.float32
    )
    cross_part = jnp.dot(
        centered, misfit_rows.T, precision=lax.Precision.HIGHEST, preferred_element_type=jnp.float32
    )
    return (gram_part, cross_part)


def sample_cells(current, sensor_offsets):
    members_here = current.shape[0]
    row_count = current.shape[1] * current.shape[2]
    width = current.shape[3]
    planes = current.reshape(members_here, row_count, width)
    slot_total = sensor_offsets.shape[0]
    block_size = math.gcd(slot_total, 512)
    block_count = slot_total // block_size
    row_ids = jnp.arange(row_count, dtype=jnp.int32)
    col_ids = jnp.arange(width, dtype=jnp.int32)

    def pick_block(offsets):
        row_pick = offsets // width
        col_pick = offsets % width
        col_table = (col_ids[:, None] == col_pick[None, :]).astype(jnp.float32)
        chosen = jnp.einsum(
            "qng,gl->qnl",
            planes,
            col_table,
            precision=lax.Precision.HIGHEST,
            preferred_element_type=jnp.float32,
        )
        row_table = (row_ids[:, None] == row_pick[None, :]).astype(jnp.float32)
        return jnp.sum(chosen * row_table[None, :, :], axis=1)

    blocks = lax.map(pick_block, sensor_offsets.reshape(block_count, block_size))
    return jnp.transpose(blocks, (1, 0, 2)).reshape(members_here, slot_total)


def local(
    fields,
    velocity,
    diffusivity,
    sensor_offsets,
    sensor_counts,
    observations,
    noise_scale,
    perturbation,
):
    members_here = fields.shape[0]
    group_count = lax.axis_size("grp")
    members_all = members_here * group_count
    spread_root = math.sqrt(members_all - 1)
    courant = velocity.astype(jnp.float32) * COURANT
    current = fields
    for counter in range(STEPS):
        extended = extended_2(current, (("slab", 1),), 1)
        current = advance(extended, courant, diffusivity)
    cell_total = current.shape[1] * current.shape[2] * current.shape[3]
    flattened = current.reshape(members_here, cell_total)
    slot_total = sensor_offsets.shape[0]
    live_mask = (jnp.arange(slot_total, dtype=jnp.int32) < sensor_counts[0]).astype(jnp.float32)
    predicted = sample_cells(current, sensor_offsets)
    scaled = live_mask * predicted / noise_scale
    misfit = live_mask * ((observations - predicted) / noise_scale + perturbation)
    scaled_sum = lax.psum(jnp.sum(scaled, axis=0), "grp")
    leading = (scaled - scaled_sum / members_all) / spread_root
    gathered_lead, gathered_misfit = (
        lax.all_gather(leading, "grp", axis=0, tiled=True),
        lax.all_gather(misfit, "grp", axis=0, tiled=True),
    )
    gram_part, cross_part = ensemble_parts(gathered_lead, gathered_misfit)
    gram_matrix, cross_matrix = lax.psum((gram_part, cross_part), "slab")
    weights = solve_weights(gram_matrix, cross_matrix, spread_root)
    group_index = lax.axis_index("grp")
    own_weights = lax.dynamic_slice_in_dim(weights, group_index * members_here, members_here, 1)
    increment = jnp.dot(
        own_weights.T,
        lax.all_gather(flattened, "grp", axis=0, tiled=True),
        precision=lax.Precision.HIGHEST,
        preferred_element_type=jnp.float32,
    )
    return (flattened + increment).reshape(current.shape)


def solution(mesh):
    return jax.shard_map(
        local,
        mesh=mesh,
        in_specs=(
            P("grp", "slab", None, None),
            P(None, "slab", None, None),
            P("slab", None, None),
            P("slab"),
            P("slab"),
            P("slab"),
            P("slab"),
            P("grp", "slab"),
        ),
        out_specs=P("grp", "slab", None, None),
        check_vma=False,
    )
```

profile of v0, /device:TPU:0, one launch (start us, length us, event | category | flops | bytes accessed | tf_op | source)
XLA Modules:
  0.0 487.9 jit_solution(3557998516879532501)
XLA Ops:
  6.5 1.6 fusion.75
  8.1 3.0 collective-permute-start
  11.1 1.3 collective-permute-start.1
  12.4 1.3 fusion.72
  13.9 1.0 fusion.74
  15.7 0.9 convert_multiply_fusion
  17.3 1.3 reshape.81
  19.9 1.4 div.111
  21.9 2.0 fusion.51
  24.5 4.6 collective-permute-start.2
  29.1 1.3 collective-permute-start.3
  30.5 3.0 collective-permute-done.3
  34.4 31.0 %while.62 = (s32[]{:T(128)}, f32[12,16,512]{2,1,0:T(8,128)S(1)}, s32[12,512]{1,0:T(8,128)}, f32[16,64,128]{2,1,0:T(8,128)S(1)}, s32[]{:T(128)}) while((s32[]{:T(128)}, f32[12,16,512]{2,1,0:T(8,128)S(1)}, s32[12,512]{1,0:T(8,128)}, f32[16,64,128]{2,1,0:T(8,128)S(1)}, s32[]{:T(128)}) %tuple.168), condition=%wide.region_2.3_spmd.clone, body=%wide.region_0.2_spmd.clone.sunk | while | flops 806489600 | bytes 901193 | solution.py:140
  35.9 1.0 fusion.109
  38.5 1.0 fusion.109
  41.1 1.0 fusion.109
  43.7 1.0 fusion.109
  46.3 1.0 fusion.109
  48.9 1.1 fusion.109
  51.5 1.0 fusion.109
  54.0 1.0 fusion.109
  56.6 1.0 fusion.109
  59.2 1.1 fusion.109
  61.8 1.0 fusion.109
  64.4 1.0 fusion.109
  65.7 16.3 %psum.21 = f32[6144]{0:T(1024)S(1)} all-reduce(f32[6144]{0:T(1024)S(1)} %reduce_sum.24), channel_id=1, replica_groups=mesh['grp'=4,'slab'=8] {'grp'}, use_global_device_ids=true, to_apply=%region_4.5 | all-reduce | flops 6144 | bytes 49152 | tf_op jit(solution)/shard_map/psum | solution.py:170
  82.0 1.0 add_multiply_fusion
  83.8 1.1 copy.20
  85.0 29.7 %all-gather.4.cloned.1.call-done = f32[64,6144]{1,0:T(8,128)} async-done(((f32[16,6144]{1,0:T(8,128)}), f32[64,6144]{1,0:T(8,128)}) %all-gather.4.cloned.1.call-update) | async-done | bytes 1572880 | tf_op jit(solution)/shard_map/all_gather | solution.py:173
  114.6 3.4 fusion.77
  118.0 29.3 %all-gather.6.cloned.1.call-done = f32[64,6144]{1,0:T(8,128)} async-done(((f32[16,6144]{1,0:T(8,128)}), f32[64,6144]{1,0:T(8,128)}) %all-gather.6.cloned.1.call-update) | async-done | bytes 1572880 | tf_op jit(solution)/shard_map/all_gather | solution.py:174
  147.3 2.8 fusion.76
  150.1 28.9 %all-reduce = (f32[64,64]{1,0:T(8,128)S(1)}, f32[64,64]{1,0:T(8,128)S(1)}) all-reduce(f32[64,64]{1,0:T(8,128)S(1)} %fusion.76, f32[64,64]{1,0:T(8,128)S(1)} %fusion.77), channel_id=1, replica_groups=mesh['grp'=4,'slab'=8] {'slab'}, use_global_device_ids=true, to_apply=%region_8.9 | all-reduce | flops 8192 | bytes 65536 | tf_op jit(solution)/shard_map/psum | solution.py:177
  179.1 105.9 %while.63 = (s32[]{:T(128)}, f32[64,64]{1,0:T(8,128)S(1)}, f32[64,64]{0,1:T(8,128)S(1)}, s32[]{:T(128)}, s32[]{:T(128)}) while((s32[]{:T(128)}, f32[64,64]{1,0:T(8,128)S(1)}, f32[64,64]{0,1:T(8,128)S(1)}, s32[]{:T(128)}, s32[]{:T(128)}) %tuple.153), condition=%wide.region_7.8_spmd.clone.clone, body=%wide.region_6.7_spmd.clone.clone.sunk | while | flops 65923 | bytes 101992 | solution.py:66
  285.1 96.0 %while.60 = (s32[]{:T(128)}, f32[64,64]{1,0:T(8,128)S(1)}, f32[64,64]{1,0:T(8,128)S(1)}, f32[64,64]{1,0:T(8,128)S(1)}, s32[]{:T(128)}, /*index=5*/s32[]{:T(128)}, s32[]{:T(128)}) while((s32[]{:T(128)}, f32[64,64]{1,0:T(8,128)S(1)}, f32[64,64]{1,0:T(8,128)S(1)}, f32[64,64]{1,0:T(8,128)S(1)}, s32[]{:T(128)}, /*index=5*/s32[]{:T(128)}, ...), condition=%wide.region_10.11_spmd, body=%wide.region_9.10_spmd.sunk | while | flops 49283 | bytes 36205 | solution.py:83
  285.8 0.8 fusion.102
  287.3 0.8 fusion.102
  288.8 0.8 fusion.102
  290.3 0.8 fusion.102
  291.8 0.8 fusion.102
  293.3 0.8 fusion.102
  294.8 0.8 fusion.102
  296.3 0.8 fusion.102
  297.8 0.8 fusion.102
  299.3 0.8 fusion.102
  381.1 96.4 %while.61 = (s32[]{:T(128)}, f32[64,64]{1,0:T(8,128)S(1)}, f32[64,64]{1,0:T(8,128)S(1)}, f32[64,64]{0,1:T(8,128)S(1)}, s32[]{:T(128)}, /*index=5*/s32[]{:T(128)}, s32[]{:T(128)}, s32[]{:T(128)}) while((s32[]{:T(128)}, f32[64,64]{1,0:T(8,128)S(1)}, f32[64,64]{1,0:T(8,128)S(1)}, f32[64,64]{0,1:T(8,128)S(1)}, s32[]{:T(128)}, ...), condition=%wide.region_12.13_spmd, body=%wide.region_11.12_spmd.sunk | while | flops 49287 | bytes 35751 | solution.py:101
  477.6 2.9 fusion.26
  480.5 0.9 copy.16
  (868 shorter events, 263.7 us)
Async XLA Ops:
  6.5 7.2 %copy-start = (f32[16,8,8,128]{3,2,1,0:T(8,128)S(1)}, f32[16,8,8,128]{3,2,1,0:T(8,128)}, u32[]{:S(2)}) copy-start(f32[16,8,8,128]{3,2,1,0:T(8,128)} %param.16) | copy-start | bytes 1572868
  6.5 108.1 %all-gather.4.cloned.1.call-start = ((), (), s32[]{:S(2)}) async-start(), calls=%async_computation | async-start | bytes 1966080 | tf_op jit(solution)/shard_map/all_gather | solution.py:173
  8.1 13.8 %collective-permute-start = (f32[16,1,8,128]{3,2,1,0:T(8,128)}, f32[16,1,8,128]{3,2,1,0:T(8,128)}, u32[]{:S(2)}, u32[]{:S(2)}) collective-permute-start(f32[16,1,8,128]{3,2,1,0:T(8,128)} %get-tuple-element.525), channel_id=1, source_target_pairs={{0,1},{1,2},{2,3},{3,4},{4,5},{5,6},{6,7},{8,9},{9,10},{10,11},{11... | collective-permute-start | bytes 196616 | tf_op jit(solution)/shard_map/ppermute | solution.py:21
  11.1 10.7 %collective-permute-start.1 = (f32[16,1,8,128]{3,2,1,0:T(8,128)}, f32[16,1,8,128]{3,2,1,0:T(8,128)}, u32[]{:S(2)}, u32[]{:S(2)}) collective-permute-start(f32[16,1,8,128]{3,2,1,0:T(8,128)} %get-tuple-element.526), channel_id=1, source_target_pairs={{1,0},{2,1},{3,2},{4,3},{5,4},{6,5},{7,6},{9,8},{10,9},{11,10},{12... | collective-permute-start | bytes 196616 | tf_op jit(solution)/shard_map/ppermute | solution.py:22
  24.2 9.3 %copy-start.3 = (f32[8,8,128]{2,1,0:T(8,128)S(1)}, f32[8,8,128]{2,1,0:T(8,128)}, u32[]{:S(2)}) copy-start(f32[8,8,128]{2,1,0:T(8,128)} %get-tuple-element.529) | copy-start | bytes 98308
  24.2 9.3 %copy-start.4 = (f32[8,8,128]{2,1,0:T(8,128)S(1)}, f32[8,8,128]{2,1,0:T(8,128)}, u32[]{:S(2)}) copy-start(f32[8,8,128]{2,1,0:T(8,128)} %get-tuple-element.530) | copy-start | bytes 98308
  24.2 9.3 %copy-start.5 = (f32[8,8,128]{2,1,0:T(8,128)S(1)}, f32[8,8,128]{2,1,0:T(8,128)}, u32[]{:S(2)}) copy-start(f32[8,8,128]{2,1,0:T(8,128)} %get-tuple-element.531) | copy-start | bytes 98308
  24.2 9.3 %copy-start.6 = (f32[8,8,128]{2,1,0:T(8,128)S(1)}, f32[8,8,128]{2,1,0:T(8,128)}, u32[]{:S(2)}) copy-start(f32[8,8,128]{2,1,0:T(8,128)} %get-tuple-element.532) | copy-start | bytes 98308
  24.3 9.3 %copy-start.7 = (f32[8,8,128]{2,1,0:T(8,128)S(1)}, f32[8,8,128]{2,1,0:T(8,128)}, u32[]{:S(2)}) copy-start(f32[8,8,128]{2,1,0:T(8,128)} %get-tuple-element.533) | copy-start | bytes 98308
  24.3 9.3 %copy-start.8 = (f32[8,8,128]{2,1,0:T(8,128)S(1)}, f32[8,8,128]{2,1,0:T(8,128)}, u32[]{:S(2)}) copy-start(f32[8,8,128]{2,1,0:T(8,128)} %get-tuple-element.534) | copy-start | bytes 98308
  24.3 9.3 %copy-start.9 = (f32[8,8,128]{2,1,0:T(8,128)S(1)}, f32[8,8,128]{2,1,0:T(8,128)}, u32[]{:S(2)}) copy-start(f32[8,8,128]{2,1,0:T(8,128)} %param.18) | copy-start | bytes 98308
  24.5 6.0 %collective-permute-start.2 = (f32[16,1,8,128]{3,2,1,0:T(8,128)S(1)}, f32[16,1,8,128]{3,2,1,0:T(8,128)S(1)}, u32[]{:S(2)}, u32[]{:S(2)}) collective-permute-start(f32[16,1,8,128]{3,2,1,0:T(8,128)S(1)} %get-tuple-element.515), channel_id=1, source_target_pairs={{0,1},{1,2},{2,3},{3,4},{4,5},{5,6},{6,7},{8,9},{9,10},{10,11},{11... | collective-permute-start | bytes 196616 | tf_op jit(solution)/shard_map/ppermute | solution.py:21
  29.1 4.4 collective-permute-start.3
  34.4 31.1 %copy-start.10 = (f32[12,512]{1,0:T(8,128)S(1)}, f32[12,512]{1,0:T(8,128)}, u32[]{:S(2)}) copy-start(f32[12,512]{1,0:T(8,128)} %fusion.61) | copy-start | bytes 73732
  34.4 31.1 %copy-start.11 = (f32[12,512]{1,0:T(8,128)S(1)}, f32[12,512]{1,0:T(8,128)}, u32[]{:S(2)}) copy-start(f32[12,512]{1,0:T(8,128)} %div.111) | copy-start | bytes 73732
  34.4 47.5 %copy-start.12 = (f32[6144]{0:T(1024)S(1)}, f32[6144]{0:T(1024)}, u32[]{:S(2)}) copy-start(f32[6144]{0:T(1024)} %param.22) | copy-start | bytes 73732
  34.4 47.5 %copy-start.13 = (f32[6144]{0:T(1024)S(1)}, f32[6144]{0:T(1024)}, u32[]{:S(2)}) copy-start(f32[6144]{0:T(1024)} %fusion.62) | copy-start | bytes 73732
  34.4 47.5 %copy-start.14 = (f32[6144]{0:T(1024)S(1)}, f32[6144]{0:T(1024)}, u32[]{:S(2)}) copy-start(f32[6144]{0:T(1024)} %param.21) | copy-start | bytes 73732
  65.5 16.5 %copy-start.2 = (f32[16,6144]{1,0:T(8,128)S(1)}, f32[16,6144]{1,0:T(8,128)}, u32[]{:S(2)}) copy-start(f32[16,6144]{1,0:T(8,128)} %param.23) | copy-start | bytes 1179652
  83.0 64.3 %all-gather.6.cloned.1.call-start = ((), (), s32[]{:S(2)}) async-start(), calls=%async_computation.1 | async-start | bytes 1966080 | tf_op jit(solution)/shard_map/all_gather | solution.py:174
  83.8 393.8 %all-gather.8.cloned.1.call-start = ((), (), s32[]{:S(2)}) async-start(), calls=%async_computation.2 | async-start | bytes 2621440 | tf_op jit(solution)/shard_map/all_gather | solution.py:183
  114.6 32.7 %copy-start.1 = (f32[64,6144]{1,0:T(8,128)S(1)}, f32[64,6144]{1,0:T(8,128)}, u32[]{:S(2)}) copy-start(f32[64,6144]{1,0:T(8,128)} %all-gather.4.cloned.1.call-done) | copy-start | bytes 4718596
Sparse Core Ops, SparseCore 0:
  83.1 31.4 all-gather.3
  116.5 30.8 all-gather.5
  149.2 35.2 all-gather.7
where the time goes:
time: 492 us; the launch traced here: 488 us
  local copies, waits for them, and re-layouts  140 us (28%)
  matrix products  134 us (27%)
  waiting for transfers between devices  62.7 us (13%)
  loops' own time  50.5 us (10%)
  blocking collectives  45.2 us (9%)
  other arithmetic  30.7 us (6%)
  between operations  14.2 us (3%)
  starting transfers between devices  10.3 us (2%)
    dot_general x64, matrix products, forward_row(): jnp.dot(factor_row, solved, precision=lax.Precision.HIGHEST, preferred_el...  51.5 us
    dot_general x64, matrix products, backward_row(): jnp.dot(factor_col, solved, precision=lax.Precision.HIGHEST, preferred_el...  51.5 us
    another operation x1, loops' own time, solve_weights(): lax.fori_loop(0, order, factor_column, jnp.zeros((order, order), jnp.floa...  47.1 us
    dynamic_slice x64, local copies, waits for them, and re-layouts, factor_column(): pivot = jnp.sqrt(lax.dynamic_slice_in_dim(needed, column, 1, 0)[0])  43.5 us
    dynamic_slice x64, local copies, waits for them, and re-layouts, forward_row(): pivot = lax.dynamic_slice_in_dim(factor_row, row, 1, 0)[0]  41.6 us
    dynamic_slice x64, local copies, waits for them, and re-layouts, backward_row(): pivot = lax.dynamic_slice_in_dim(factor_col, row, 1, 0)[0]  41.6 us
    all_gather x1, waiting for transfers between devices, local(): lax.all_gather(leading, 'grp', axis=0, tiled=True)  29.7 us
    all_gather x1, waiting for transfers between devices, local(): lax.all_gather(misfit, 'grp', axis=0, tiled=True)  29.3 us
  transfers between devices with their start and end apart: 7, of which 3 were waited for; matrix products, arithmetic and copies ran while one was open for 54% of the time, Pallas kernels for 0%

commit v1 on v0

v1 whole, which is shorter than its diff:
```python
import functools

import jax
import jax.numpy as jnp
from jax import lax
from jax.experimental import pallas as pl
from jax.experimental.pallas import tpu as pltpu
from jax.sharding import PartitionSpec as P

STEPS = 2
COURANT = 0.12
LANES = 128
BLOCK = 8
MESH = pl.DeviceIdType.MESH
NT = (((1,), (1,)), ((), ()))
TN = (((0,), (0,)), ((), ()))


def split_two(values):
    high = values.astype(jnp.bfloat16).astype(jnp.float32)
    return high, values - high


def scatter_kernel(groups, count_ref, off_ref, obs_ref, noise_ref, pert_ref, v_ref, w_ref, bt, a2):
    members, slots = pert_ref.shape
    width = bt.shape[0]
    high_count = w_ref.shape[1]
    per_group = high_count // groups
    off = off_ref[...]
    low = off % width
    high = off // width
    slot = lax.broadcasted_iota(jnp.int32, (1, slots), 1)
    noise = noise_ref[...]
    inverse = jnp.where(slot < count_ref[0], 1.0 / noise, 0.0)
    rows = lax.broadcasted_iota(jnp.int32, (width, slots), 0)
    bt[...] = jnp.where(rows == low, 1.0, 0.0).astype(jnp.bfloat16)
    one = bt[...]

    value = (obs_ref[...] / noise + pert_ref[...]) * inverse
    first, second = split_two(value)
    both = jnp.concatenate([first, second], axis=0)

    def group(q, carry):
        for k in range(per_group):
            a2[k * 2 * members : (k + 1) * 2 * members, :] = jnp.where(
                high == q * per_group + k, both, 0.0
            ).astype(jnp.bfloat16)
        res = lax.dot_general(a2[...], bt[...], NT, preferred_element_type=jnp.float32)
        for k in range(per_group):
            part = res[2 * k * members : (2 * k + 1) * members] + res[
                (2 * k + 1) * members : (2 * k + 2) * members
            ]
            for i in range(width // LANES):
                v_ref[(q * per_group + k) * (width // LANES) + i] = part[
                    :, i * LANES : (i + 1) * LANES
                ]
        return carry

    lax.fori_loop(0, groups, group, 0)

    weight = inverse * inverse
    high_rows = lax.broadcasted_iota(jnp.int32, (high_count, slots), 0)
    first, second = split_two(jnp.where(high_rows == high, weight, 0.0))
    stacked = jnp.concatenate([first, second], axis=0).astype(jnp.bfloat16)
    res = lax.dot_general(stacked, one, NT, preferred_element_type=jnp.float32)
    total = res[:high_count] + res[high_count:]
    for i in range(width // LANES):
        w_ref[i] = total[:, i * LANES : (i + 1) * LANES]


def scatter_terms(groups, units, counts, offsets, observations, noise, perturbation):
    members, slots = perturbation.shape
    width = 2 * LANES
    high_count = units * LANES // width
    vmem = pl.BlockSpec(memory_space=pltpu.VMEM)
    return pl.pallas_call(
        functools.partial(scatter_kernel, groups),
        out_shape=(
            jax.ShapeDtypeStruct((units, members, LANES), jnp.float32),
            jax.ShapeDtypeStruct((width // LANES, high_count, LANES), jnp.float32),
        ),
        in_specs=[pl.BlockSpec(memory_space=pltpu.SMEM)] + [vmem] * 4,
        out_specs=(vmem, vmem),
        scratch_shapes=[
            pltpu.VMEM((width, slots), jnp.bfloat16),
            pltpu.VMEM((high_count // groups * 2 * members, slots), jnp.bfloat16),
        ],
        compiler_params=pltpu.CompilerParams(vmem_limit_bytes=48 * 1024 * 1024),
        name="scatter_terms",
    )(counts, offsets[None], observations[None], noise[None], perturbation)


def upwind(courant, center, lower_side, upper_side):
    return jnp.maximum(courant, 0.0) * (center - lower_side) + jnp.minimum(courant, 0.0) * (
        upper_side - center
    )


def advance(below, center, above, cz, cy, cx, diffusivity):
    y_size, x_size = center.shape[1:]
    south = pltpu.roll(center, 1, 1)
    north = pltpu.roll(center, y_size - 1, 1)
    west = pltpu.roll(center, 1, 2)
    east = pltpu.roll(center, x_size - 1, 2)
    transport = upwind(cz, center, below, above) + upwind(cy, center, south, north)
    transport = transport + upwind(cx, center, west, east)
    laplace = below + above + south + north + west + east - 6.0 * center
    return center - transport + diffusivity * laplace


def solve_in_place(m_ref):
    order, width = m_ref.shape

    def block(b, carry):
        start = pl.multiple_of(b * BLOCK, BLOCK)
        whole = m_ref[...]
        rows = m_ref[pl.ds(start, BLOCK), :]
        row_id = lax.broadcasted_iota(jnp.int32, (BLOCK, width), 0)
        cols = [jnp.broadcast_to(rows[:, i : i + 1], (BLOCK, width)) for i in range(BLOCK)]
        for j in range(BLOCK):
            inverse = 1.0 / cols[j][j : j + 1, :]
            mine = cols[j]
            here = row_id == j

            def eliminate(t):
                pivot_row = t[j : j + 1, :] * inverse
                return jnp.where(here, pivot_row, t - mine * pivot_row)

            rows = eliminate(rows)
            for i in range(j + 1, BLOCK):
                cols[i] = eliminate(cols[i])
        new = whole
        for j in range(BLOCK):
            new = new - whole[:, j : j + 1] * rows[j : j + 1, :]
        m_ref[...] = pltpu.roll(new, width - BLOCK, 1)
        m_ref[pl.ds(start, BLOCK), :] = pltpu.roll(rows, width - BLOCK, 1)
        return carry

    lax.fori_loop(0, order // BLOCK, block, 0)


def step_kernel(
    groups,
    slabs,
    v_ref,
    w_ref,
    fields_ref,
    vel_ref,
    dif_ref,
    out_ref,
    ext,
    velx,
    difx,
    mid,
    own,
    eq,
    vq,
    xs,
    xc,
    yz,
    part,
    rs,
    rowsum,
    rg,
    total,
    m_ref,
    upd,
    ret,
    halo_send,
    halo_recv,
    gs_sem,
    gr_sem,
    ss_sem,
    sr_sem,
):
    g, s = lax.axis_index("grp"), lax.axis_index("slab")
    members, planes, ys, xsz = fields_ref.shape
    units = planes * ys
    per = units // groups
    order = members * groups
    depth = order // slabs

    barrier = pltpu.get_barrier_semaphore()
    for r in range(1, groups):
        pl.semaphore_signal(
            barrier, inc=1, device_id=(lax.rem(g + r, groups), s), device_id_type=MESH
        )
    for r in range(1, slabs):
        pl.semaphore_signal(
            barrier, inc=1, device_id=(g, lax.rem(s + r, slabs)), device_id_type=MESH
        )
    pl.semaphore_wait(barrier, groups + slabs - 2)

    def halo(sign, k, src, dst):
        return pltpu.make_async_remote_copy(
            src_ref=src,
            dst_ref=dst,
            send_sem=halo_send.at[(sign + 1) // 2, k],
            recv_sem=halo_recv.at[(sign + 1) // 2, k],
            device_id=(g, lax.rem(s + sign + slabs, slabs)),
            device_id_type=MESH,
        )

    last = planes + STEPS
    up = [
        halo(1, 0, fields_ref.at[:, planes - 2 : planes], ext.at[:, 0:2]),
        halo(1, 1, vel_ref.at[:, planes - 1 : planes], velx.at[:, 0:1]),
        halo(1, 2, dif_ref.at[planes - 1 : planes], difx.at[0:1]),
    ]
    down = [
        halo(-1, 0, fields_ref.at[:, 0:2], ext.at[:, last : last + 2]),
        halo(-1, 1, vel_ref.at[:, 0:1], velx.at[:, planes + 1 : planes + 2]),
        halo(-1, 2, dif_ref.at[0:1], difx.at[planes + 1 : planes + 2]),
    ]

    @pl.when(s < slabs - 1)
    def _():
        for copy in up:
            copy.start()

    @pl.when(s > 0)
    def _():
        for copy in down:
            copy.start()

    def grp_copy(phase, r, src, dst):
        return pltpu.make_async_remote_copy(
            src_ref=src,
            dst_ref=dst,
            send_sem=gs_sem.at[phase, r],
            recv_sem=gr_sem.at[phase, r],
            device_id=(lax.rem(g + r, groups), s),
            device_id_type=MESH,
        )

    def slab_copy(phase, r, src, dst):
        return pltpu.make_async_remote_copy(
            src_ref=src,
            dst_ref=dst,
            send_sem=ss_sem.at[phase, r],
            recv_sem=sr_sem.at[phase, r],
            device_id=(g, lax.rem(s + r, slabs)),
            device_id_type=MESH,
        )

    def units_of(r):
        return pl.ds(lax.rem(g + r, groups) * per, per)

    v_copies = [
        grp_copy(0, r, v_ref.at[units_of(r)], vq.at[g]) for r in range(1, groups)
    ]
    for copy in v_copies:
        copy.start()
    vq[g] = v_ref[units_of(0)]

    ext[:, 2:last] = fields_ref[...]
    velx[:, 1 : planes + 1] = vel_ref[...]
    difx[1 : planes + 1] = dif_ref[...]

    @pl.when(s == 0)
    def _():
        ext[:, 0:2] = jnp.zeros((members, 2, ys, xsz), jnp.float32)
        velx[:, 0:1] = jnp.zeros((3, 1, ys, xsz), jnp.int32)
        difx[0:1] = jnp.zeros((1, ys, xsz), jnp.float32)

    @pl.when(s == slabs - 1)
    def _():
        ext[:, last : last + 2] = jnp.zeros((members, 2, ys, xsz), jnp.float32)
        velx[:, planes + 1 : planes + 2] = jnp.zeros((3, 1, ys, xsz), jnp.int32)
        difx[planes + 1 : planes + 2] = jnp.zeros((1, ys, xsz), jnp.float32)

    @pl.when(s > 0)
    def _():
        for copy in up:
            copy.wait_recv()

    @pl.when(s < slabs - 1)
    def _():
        for copy in down:
            copy.wait_recv()

    def coefficients(p):
        courant = [velx[c, p].astype(jnp.float32)[None] * COURANT for c in range(3)]
        return courant + [difx[p][None]]

    def first_step(p, carry):
        mid[:, p] = advance(ext[:, p], ext[:, p + 1], ext[:, p + 2], *coefficients(p))
        return carry

    lax.fori_loop(0, planes + 2, first_step, 0)

    @pl.when(s == 0)
    def _():
        mid[:, 0] = jnp.zeros((members, ys, xsz), jnp.float32)

    @pl.when(s == slabs - 1)
    def _():
        mid[:, planes + 1] = jnp.zeros((members, ys, xsz), jnp.float32)

    def second_step(p, carry):
        res = advance(mid[:, p], mid[:, p + 1], mid[:, p + 2], *coefficients(p + 1))
        own[pl.ds(p * ys, ys)] = jnp.swapaxes(res, 0, 1)
        return carry

    lax.fori_loop(0, planes, second_step, 0)

    e_copies = [grp_copy(1, r, own.at[units_of(r)], eq.at[g]) for r in range(1, groups)]
    for copy in e_copies:
        copy.start()
    eq[g] = own[units_of(0)]
    for copy in v_copies:
        copy.wait_recv()
    for copy in e_copies:
        copy.wait_recv()

    per_row = w_ref.shape[0]
    first_row = g * (per // per_row)
    for u in range(per):
        lanes = slice(u * LANES, (u + 1) * LANES)
        x = jnp.concatenate([eq[q, u] for q in range(groups)], axis=0)
        v = jnp.concatenate([vq[q, u] for q in range(groups)], axis=0)
        w = w_ref[u % per_row, pl.ds(first_row + u // per_row, 1), :]
        centered = x - jnp.sum(x, axis=0, keepdims=True) / order
        xs[:, lanes] = x
        xc[:, lanes] = centered
        yz[0:order, lanes] = centered * w
        yz[order : 2 * order, lanes] = v - x * w
    part[...] = lax.dot_general(
        xc[...],
        yz[...],
        NT,
        precision=lax.Precision.HIGHEST,
        preferred_element_type=jnp.float32,
    ) / (order - 1)

    def rows_of(r):
        return pl.ds(pl.multiple_of(lax.rem(s + r, slabs) * depth, depth), depth)

    rs_copies = [slab_copy(0, r, part.at[rows_of(r)], rs.at[s]) for r in range(1, slabs)]
    for copy in rs_copies:
        copy.start()
    rs[s] = part[rows_of(0), :]
    for copy in rs_copies:
        copy.wait_recv()
    added = rs[0]
    for i in range(1, slabs):
        added = added + rs[i]
    rowsum[...] = added
    rg_copies = [grp_copy(2, r, rowsum, rg.at[g]) for r in range(1, groups)]
    for copy in rg_copies:
        copy.start()
    rg[g] = added
    for copy in rg_copies:
        copy.wait_recv()
    added = rg[0]
    for i in range(1, groups):
        added = added + rg[i]
    total[...] = added
    ag_copies = [slab_copy(1, r, total, m_ref.at[rows_of(0)]) for r in range(1, slabs)]
    for copy in ag_copies:
        copy.start()
    m_ref[rows_of(0), :] = added
    for copy in ag_copies:
        copy.wait_recv()

    shape = m_ref.shape
    diagonal = lax.broadcasted_iota(jnp.int32, shape, 0) == lax.broadcasted_iota(
        jnp.int32, shape, 1
    )
    m_ref[...] = m_ref[...] + jnp.where(diagonal, 1.0, 0.0)
    solve_in_place(m_ref)

    new = xs[...] + lax.dot_general(
        m_ref[:, 0:order],
        xs[...],
        TN,
        precision=lax.Precision.HIGHEST,
        preferred_element_type=jnp.float32,
    )
    for q in range(groups):
        for u in range(per):
            upd[q, u] = new[q * members : (q + 1) * members, u * LANES : (u + 1) * LANES]
    u_copies = [
        grp_copy(3, r, upd.at[lax.rem(g + r, groups)], ret.at[units_of(0)])
        for r in range(1, groups)
    ]
    for copy in u_copies:
        copy.start()
    ret[units_of(0)] = upd[g]
    for copy in u_copies:
        copy.wait_recv()

    def finish(p, carry):
        out_ref[:, p] = jnp.swapaxes(ret[pl.ds(p * ys, ys)], 0, 1)
        return carry

    lax.fori_loop(0, planes, finish, 0)

    for copy in v_copies + e_copies + rs_copies + rg_copies + ag_copies + u_copies:
        copy.wait_send()

    @pl.when(s < slabs - 1)
    def _():
        for copy in up:
            copy.wait_send()

    @pl.when(s > 0)
    def _():
        for copy in down:
            copy.wait_send()


def local(
    groups,
    slabs,
    fields,
    velocity,
    diffusivity,
    sensor_offsets,
    sensor_counts,
    observations,
    noise_scale,
    perturbation,
):
    members, planes, ys, xsz = fields.shape
    units = planes * ys
    per = units // groups
    order = members * groups
    depth = order // slabs
    terms, weight = scatter_terms(
        groups, units, sensor_counts, sensor_offsets, observations, noise_scale, perturbation
    )
    vmem = pl.BlockSpec(memory_space=pltpu.VMEM)
    f32 = jnp.float32
    scratch = [
        pltpu.VMEM((members, planes + 4, ys, xsz), f32),
        pltpu.VMEM((3, planes + 2, ys, xsz), jnp.int32),
        pltpu.VMEM((planes + 2, ys, xsz), f32),
        pltpu.VMEM((members, planes + 2, ys, xsz), f32),
        pltpu.VMEM((units, members, xsz), f32),
        pltpu.VMEM((groups, per, members, xsz), f32),
        pltpu.VMEM((groups, per, members, xsz), f32),
        pltpu.VMEM((order, per * xsz), f32),
        pltpu.VMEM((order, per * xsz), f32),
        pltpu.VMEM((2 * order, per * xsz), f32),
        pltpu.VMEM((order, 2 * order), f32),
        pltpu.VMEM((slabs, depth, 2 * order), f32),
        pltpu.VMEM((depth, 2 * order), f32),
        pltpu.VMEM((groups, depth, 2 * order), f32),
        pltpu.VMEM((depth, 2 * order), f32),
        pltpu.VMEM((order, 2 * order), f32),
        pltpu.VMEM((groups, per, members, xsz), f32),
        pltpu.VMEM((units, members, xsz), f32),
        pltpu.SemaphoreType.DMA((2, 3)),
        pltpu.SemaphoreType.DMA((2, 3)),
        pltpu.SemaphoreType.DMA((4, groups)),
        pltpu.SemaphoreType.DMA((4, groups)),
        pltpu.SemaphoreType.DMA((2, slabs)),
        pltpu.SemaphoreType.DMA((2, slabs)),
    ]
    return pl.pallas_call(
        functools.partial(step_kernel, groups, slabs),
        out_shape=jax.ShapeDtypeStruct(fields.shape, f32),
        in_specs=[vmem] * 5,
        out_specs=vmem,
        scratch_shapes=scratch,
        compiler_params=pltpu.CompilerParams(
            collective_id=0, has_side_effects=True, vmem_limit_bytes=56 * 1024 * 1024
        ),
        name="ensemble_step",
    )(terms, weight, fields, velocity, diffusivity)


def solution(mesh):
    return jax.shard_map(
        functools.partial(local, mesh.shape["grp"], mesh.shape["slab"]),
        mesh=mesh,
        in_specs=(
            P("grp", "slab", None, None),
            P(None, "slab", None, None),
            P("slab", None, None),
            P("slab"),
            P("slab"),
            P("slab"),
            P("slab"),
            P("grp", "slab"),
        ),
        out_specs=P("grp", "slab", None, None),
        check_vma=False,
    )
```

time: 492 us -> 60.1 us (0.12)
  matrix products: 134 us -> 0 us
  local copies, waits for them, and re-layouts: 140 us -> 6.51 us
  waiting for transfers between devices: 62.7 us -> 0 us
  Pallas kernels: 0 us -> 52.5 us
  loops' own time: 50.5 us -> 0 us
  blocking collectives: 45.2 us -> 0 us
  other arithmetic: 30.7 us -> 0 us
  between operations: 14.2 us -> 0.68 us
  starting transfers between devices: 10.3 us -> 0 us
    dot_general x207 -> x0, matrix products: 134 us -> none  [the longest x64 51.5 us: forward_row(): jnp.dot(factor_row, solved, precision=lax.Precision.HIGHEST, preferred_el...]
    dynamic_slice x192 -> x0, local copies, waits for them, and re-layouts: 127 us -> none  [the longest x64 43.5 us: factor_column(): pivot = jnp.sqrt(lax.dynamic_slice_in_dim(needed, column, 1, 0)[0])]
    all_gather x3 -> x0, waiting for transfers between devices: 59 us -> none  [the longest x1 29.7 us: local(): lax.all_gather(leading, 'grp', axis=0, tiled=True)]
    pallas_call x0 -> x2, Pallas kernels: none -> 52.5 us  [the longest x1 44.5 us: local(): pl.pallas_call(functools.partial(step_kernel, groups, slabs), out_shape=j...]
    another operation x4 -> x0, loops' own time: 50.5 us -> none  [the longest x1 47.1 us: solve_weights(): lax.fori_loop(0, order, factor_column, jnp.zeros((order, order), jnp.floa...]
    psum x2 -> x0, blocking collectives: 45.2 us -> none  [the longest x1 28.9 us: local(): gram_matrix, cross_matrix = lax.psum((gram_part, cross_part), 'slab')]
    select_n x88 -> x0, other arithmetic: 18.1 us -> none  [the longest x12 8.87 us: pick_block(): row_pick = offsets // width]
    ppermute x4 -> x0, starting transfers between devices: 10.2 us -> none  [the longest x2 7.62 us: extended_2(): before = lax.ppermute(last, axis, up)]
  transfers between devices with their start and end apart: 7 -> 0, of which waited for: 3 -> 0; matrix products, arithmetic and copies ran while one was open for 54% -> 0% of each run, Pallas kernels for 0% -> 0%
where the time goes in v1:
time: 60.1 us; the launch traced here: 59.7 us
  Pallas kernels  52.5 us (87%)
  local copies, waits for them, and re-layouts  6.51 us (11%)
  between operations  0.68 us (1%)
    pallas_call x1, Pallas kernels, local(): pl.pallas_call(functools.partial(step_kernel, groups, slabs), out_shape=j...  44.5 us
    pallas_call x1, Pallas kernels, scatter_terms(): pl.pallas_call(functools.partial(scatter_kernel, groups), out_shape=(jax....  8 us
    unnamed x13, local copies, waits for them, and re-layouts  6.51 us

profile of v1, /device:TPU:0, one launch (start us, length us, event | category | flops | bytes accessed | tf_op | source)
XLA Modules:
  0.0 59.7 jit_solution(8208546277826635037)
XLA Ops:
  0.7 0.0 copy-start.1
  0.7 1.0 %copy-done.1 = f32[16,6144]{1,0:T(8,128)S(1)} copy-done((f32[16,6144]{1,0:T(8,128)S(1)}, f32[16,6144]{1,0:T(8,128)}, u32[]{:S(2)}) %copy-start.1) | copy-done | bytes 393240
  1.6 0.0 copy-start.3
  1.7 0.7 %copy-done.3 = s32[6144]{0:T(1024)S(1)} copy-done((s32[6144]{0:T(1024)S(1)}, s32[6144]{0:T(1024)}, u32[]{:S(2)}) %copy-start.3) | copy-done | bytes 24600
  2.4 0.0 copy-start.4
  2.4 0.7 %copy-done.4 = f32[6144]{0:T(1024)S(1)} copy-done((f32[6144]{0:T(1024)S(1)}, f32[6144]{0:T(1024)}, u32[]{:S(2)}) %copy-start.4) | copy-done | bytes 24600
  3.1 0.0 copy-start.5
  3.1 0.7 %copy-done.5 = f32[6144]{0:T(1024)S(1)} copy-done((f32[6144]{0:T(1024)S(1)}, f32[6144]{0:T(1024)}, u32[]{:S(2)}) %copy-start.5) | copy-done | bytes 24600
  3.9 8.0 %scatter_terms.1 = (f32[64,16,128]{2,1,0:T(8,128)S(1)}, f32[2,32,128]{2,1,0:T(8,128)S(1)}) custom-call(s32[1]{0:T(128)S(6)} %copy.10.count_ref, s32[1,6144]{1,0:T(1,128)S(1)} %bitcast.3, f32[1,6144]{1,0:T(1,128)S(1)} %bitcast.4, f32[1,6144]{1,0:T(1,128)S(1)} %bitcast.5, f32[16,6144]{1,0:T(8,128)S(1)} %copy-done.1), custom_call_target="tpu_custom_call" | custom-call | tf_op jit(solution)/shard_map/scatter_terms/pallas_call | solution.py:76
  11.9 0.0 copy-start
  11.9 0.8 %copy-done = f32[64,16,128]{2,1,0:T(8,128)} copy-done((f32[64,16,128]{2,1,0:T(8,128)}, f32[64,16,128]{2,1,0:T(8,128)S(1)}, u32[]{:S(2)}) %copy-start) | copy-done | bytes 524312
  12.7 0.0 copy-start.2
  12.7 0.6 %copy-done.2 = f32[2,32,128]{2,1,0:T(8,128)} copy-done((f32[2,32,128]{2,1,0:T(8,128)}, f32[2,32,128]{2,1,0:T(8,128)S(1)}, u32[]{:S(2)}) %copy-start.2) | copy-done | bytes 32792
  13.3 44.5 %ensemble_step.1 = f32[16,8,8,128]{3,2,1,0:T(8,128)} custom-call(f32[64,16,128]{2,1,0:T(8,128)} %copy-done, f32[2,32,128]{2,1,0:T(8,128)} %copy-done.2, f32[16,8,8,128]{3,2,1,0:T(8,128)} %fields_ref.1, s32[3,8,8,128]{3,2,1,0:T(8,128)} %vel_ref.1, f32[8,8,128]{2,1,0:T(8,128)} %dif_ref.1), custom_call_target="tpu_custom_call" | custom-call | tf_op jit(solution)/shard_map/ensemble_step/pallas_call | solution.py:461
  57.8 1.9 %copy.11 = f32[16,8,8,128]{3,2,1,0:T(8,128)} copy(f32[16,8,8,128]{3,2,1,0:T(8,128)} %ensemble_step.1) | data formatting | bytes 1048576
Async XLA Ops:
  0.7 1.0 %copy-start.1 = (f32[16,6144]{1,0:T(8,128)S(1)}, f32[16,6144]{1,0:T(8,128)}, u32[]{:S(2)}) copy-start(f32[16,6144]{1,0:T(8,128)} %pert_ref.1) | copy-start | bytes 1179652
  1.6 0.7 %copy-start.3 = (s32[6144]{0:T(1024)S(1)}, s32[6144]{0:T(1024)}, u32[]{:S(2)}) copy-start(s32[6144]{0:T(1024)} %param.11) | copy-start | bytes 73732
  2.4 0.7 %copy-start.4 = (f32[6144]{0:T(1024)S(1)}, f32[6144]{0:T(1024)}, u32[]{:S(2)}) copy-start(f32[6144]{0:T(1024)} %param.13) | copy-start | bytes 73732
  3.1 0.7 %copy-start.5 = (f32[6144]{0:T(1024)S(1)}, f32[6144]{0:T(1024)}, u32[]{:S(2)}) copy-start(f32[6144]{0:T(1024)} %param.14) | copy-start | bytes 73732
  11.9 0.8 %copy-start = (f32[64,16,128]{2,1,0:T(8,128)}, f32[64,16,128]{2,1,0:T(8,128)S(1)}, u32[]{:S(2)}) copy-start(f32[64,16,128]{2,1,0:T(8,128)S(1)} %get-tuple-element.7.v_ref) | copy-start | bytes 1572868
  12.7 0.6 %copy-start.2 = (f32[2,32,128]{2,1,0:T(8,128)}, f32[2,32,128]{2,1,0:T(8,128)S(1)}, u32[]{:S(2)}) copy-start(f32[2,32,128]{2,1,0:T(8,128)S(1)} %get-tuple-element.8.w_ref) | copy-start | bytes 98308

commit v2 on v1

--- a/solution.py
+++ b/solution.py
@@ -9,6 +9,7 @@
 
 STEPS = 2
 COURANT = 0.12
+EARLY = 3
 LANES = 128
 BLOCK = 8
 MESH = pl.DeviceIdType.MESH
@@ -21,73 +22,36 @@
     return high, values - high
 
 
-def scatter_kernel(groups, count_ref, off_ref, obs_ref, noise_ref, pert_ref, v_ref, w_ref, bt, a2):
-    members, slots = pert_ref.shape
-    width = bt.shape[0]
-    high_count = w_ref.shape[1]
-    per_group = high_count // groups
-    off = off_ref[...]
-    low = off % width
-    high = off // width
-    slot = lax.broadcasted_iota(jnp.int32, (1, slots), 1)
-    noise = noise_ref[...]
-    inverse = jnp.where(slot < count_ref[0], 1.0 / noise, 0.0)
-    rows = lax.broadcasted_iota(jnp.int32, (width, slots), 0)
-    bt[...] = jnp.where(rows == low, 1.0, 0.0).astype(jnp.bfloat16)
-    one = bt[...]
-
-    value = (obs_ref[...] / noise + pert_ref[...]) * inverse
-    first, second = split_two(value)
-    both = jnp.concatenate([first, second], axis=0)
-
-    def group(q, carry):
-        for k in range(per_group):
-            a2[k * 2 * members : (k + 1) * 2 * members, :] = jnp.where(
-                high == q * per_group + k, both, 0.0
-            ).astype(jnp.bfloat16)
-        res = lax.dot_general(a2[...], bt[...], NT, preferred_element_type=jnp.float32)
-        for k in range(per_group):
-            part = res[2 * k * members : (2 * k + 1) * members] + res[
-                (2 * k + 1) * members : (2 * k + 2) * members
-            ]
-            for i in range(width // LANES):
-                v_ref[(q * per_group + k) * (width // LANES) + i] = part[
-                    :, i * LANES : (i + 1) * LANES
-                ]
-        return carry
-
-    lax.fori_loop(0, groups, group, 0)
-
-    weight = inverse * inverse
-    high_rows = lax.broadcasted_iota(jnp.int32, (high_count, slots), 0)
-    first, second = split_two(jnp.where(high_rows == high, weight, 0.0))
+def spread_low(bt, off):
+    rows = lax.broadcasted_iota(jnp.int32, bt.shape, 0)
+    bt[...] = jnp.where(rows == off % bt.shape[0], 1.0, 0.0).astype(jnp.bfloat16)
+
+
+def scatter_group(q, high, both, bt, a2, store):
+    members = both.shape[0] // 2
+    per_group = a2.shape[0] // (2 * members)
+    ratio = bt.shape[0] // LANES
+    for k in range(per_group):
+        a2[k * 2 * members : (k + 1) * 2 * members, :] = jnp.where(
+            high[...] == q * per_group + k, both[...], 0.0
+        ).astype(jnp.bfloat16)
+    res = lax.dot_general(a2[...], bt[...], NT, preferred_element_type=jnp.float32)
+    for k in range(per_group):
+        start = 2 * k * members
+        added = res[start : start + members] + res[start + members : start + 2 * members]
+        for i in range(ratio):
+            store(k * ratio + i, added[:, i * LANES : (i + 1) * LANES])
+
+
+def scatter_weights(g, per_group, high, weight, bt, w_ref):
+    rows = w_ref.shape[1]
+    wanted = lax.broadcasted_iota(jnp.int32, (rows, high.shape[1]), 0) + g * per_group
+    first, second = split_two(jnp.where(wanted == high[...], weight, 0.0))
     stacked = jnp.concatenate([first, second], axis=0).astype(jnp.bfloat16)
-    res = lax.dot_general(stacked, one, NT, preferred_element_type=jnp.float32)
-    total = res[:high_count] + res[high_count:]
-    for i in range(width // LANES):
+    res = lax.dot_general(stacked, bt[...], NT, preferred_element_type=jnp.float32)
+    total = res[:rows] + res[rows:]
+    for i in range(w_ref.shape[0]):
         w_ref[i] = total[:, i * LANES : (i + 1) * LANES]
-
-
-def scatter_terms(groups, units, counts, offsets, observations, noise, perturbation):
-    members, slots = perturbation.shape
-    width = 2 * LANES
-    high_count = units * LANES // width
-    vmem = pl.BlockSpec(memory_space=pltpu.VMEM)
-    return pl.pallas_call(
-        functools.partial(scatter_kernel, groups),
-        out_shape=(
-            jax.ShapeDtypeStruct((units, members, LANES), jnp.float32),
-            jax.ShapeDtypeStruct((width // LANES, high_count, LANES), jnp.float32),
-        ),
-        in_specs=[pl.BlockSpec(memory_space=pltpu.SMEM)] + [vmem] * 4,
-        out_specs=(vmem, vmem),
-        scratch_shapes=[
-            pltpu.VMEM((width, slots), jnp.bfloat16),
-            pltpu.VMEM((high_count // groups * 2 * members, slots), jnp.bfloat16),
-        ],
-        compiler_params=pltpu.CompilerParams(vmem_limit_bytes=48 * 1024 * 1024),
-        name="scatter_terms",
-    )(counts, offsets[None], observations[None], noise[None], perturbation)
 
 
 def upwind(courant, center, lower_side, upper_side):
@@ -142,12 +106,24 @@
 def step_kernel(
     groups,
     slabs,
-    v_ref,
-    w_ref,
+    count_ref,
+    off_hbm,
+    obs_hbm,
+    noise_hbm,
+    pert_hbm,
     fields_ref,
     vel_ref,
     dif_ref,
-    out_ref,
+    ret,
+    off_ref,
+    obs_ref,
+    noise_ref,
+    pert_ref,
+    bt,
+    a2,
+    both,
+    v_ref,
+    w_ref,
     ext,
     velx,
     difx,
@@ -165,7 +141,7 @@
     total,
     m_ref,
     upd,
-    ret,
+    local_sem,
     halo_send,
     halo_recv,
     gs_sem,
@@ -179,6 +155,24 @@
     per = units // groups
     order = members * groups
     depth = order // slabs
+    last = planes + STEPS
+
+    loads = [
+        pltpu.make_async_copy(source, target, local_sem.at[i])
+        for i, (source, target) in enumerate(
+            (
+                (off_hbm, off_ref),
+                (noise_hbm, noise_ref),
+                (obs_hbm, obs_ref),
+                (pert_hbm, pert_ref),
+                (fields_ref, ext.at[:, 2:last]),
+                (vel_ref, velx.at[:, 1 : planes + 1]),
+                (dif_ref, difx.at[1 : planes + 1]),
+            )
+        )
+    ]
+    for copy in loads:
+        copy.start()
 
     barrier = pltpu.get_barrier_semaphore()
     for r in range(1, groups):
@@ -189,6 +183,8 @@
         pl.semaphore_signal(
             barrier, inc=1, device_id=(g, lax.rem(s + r, slabs)), device_id_type=MESH
         )
+    loads[0].wait()
+    spread_low(bt, off_ref[...])
     pl.semaphore_wait(barrier, groups + slabs - 2)
 
     def halo(sign, k, src, dst):
@@ -201,7 +197,6 @@
             device_id_type=MESH,
         )
 
-    last = planes + STEPS
     up = [
         halo(1, 0, fields_ref.at[:, planes - 2 : planes], ext.at[:, 0:2]),
         halo(1, 1, vel_ref.at[:, planes - 1 : planes], velx.at[:, 0:1]),
@@ -246,16 +241,37 @@
     def units_of(r):
         return pl.ds(lax.rem(g + r, groups) * per, per)
 
-    v_copies = [
-        grp_copy(0, r, v_ref.at[units_of(r)], vq.at[g]) for r in range(1, groups)
-    ]
-    for copy in v_copies:
-        copy.start()
-    vq[g] = v_ref[units_of(0)]
-
-    ext[:, 2:last] = fields_ref[...]
-    velx[:, 1 : planes + 1] = vel_ref[...]
-    difx[1 : planes + 1] = dif_ref[...]
+    for copy in loads[1:4]:
+        copy.wait()
+    noise = noise_ref[...]
+    slot = lax.broadcasted_iota(jnp.int32, noise.shape, 1)
+    inverse = jnp.where(slot < count_ref[0], 1.0 / noise, 0.0)
+    first, second = split_two((obs_ref[...] / noise + pert_ref[...]) * inverse)
+    both[0:members, :] = first
+    both[members : 2 * members, :] = second
+    off_ref[...] = off_ref[...] // bt.shape[0]
+
+    def v_copy(r):
+        return grp_copy(0, r, v_ref.at[units_of(r)], vq.at[g])
+
+    def scatter_turn(r, carry):
+        q = lax.rem(g + r, groups)
+
+        def store(u, value):
+            v_ref[q * per + u] = value
+
+        scatter_group(q, off_ref, both, bt, a2, store)
+
+        @pl.when(r < groups)
+        def _():
+            v_copy(r).start()
+
+        return carry
+
+    lax.fori_loop(1, EARLY, scatter_turn, 0)
+
+    for copy in loads[4:]:
+        copy.wait()
 
     @pl.when(s == 0)
     def _():
@@ -308,18 +324,21 @@
     for copy in e_copies:
         copy.start()
     eq[g] = own[units_of(0)]
+    lax.fori_loop(EARLY, groups + 1, scatter_turn, 0)
+    vq[g] = v_ref[units_of(0)]
+    scatter_weights(g, per // (bt.shape[0] // LANES), off_ref, inverse * inverse, bt, w_ref)
+    v_copies = [v_copy(r) for r in range(1, groups)]
     for copy in v_copies:
         copy.wait_recv()
     for copy in e_copies:
         copy.wait_recv()
 
     per_row = w_ref.shape[0]
-    first_row = g * (per // per_row)
     for u in range(per):
         lanes = slice(u * LANES, (u + 1) * LANES)
         x = jnp.concatenate([eq[q, u] for q in range(groups)], axis=0)
         v = jnp.concatenate([vq[q, u] for q in range(groups)], axis=0)
-        w = w_ref[u % per_row, pl.ds(first_row + u // per_row, 1), :]
+        w = w_ref[u % per_row, u // per_row : u // per_row + 1, :]
         centered = x - jnp.sum(x, axis=0, keepdims=True) / order
         xs[:, lanes] = x
         xc[:, lanes] = centered
@@ -390,12 +409,6 @@
     for copy in u_copies:
         copy.wait_recv()
 
-    def finish(p, carry):
-        out_ref[:, p] = jnp.swapaxes(ret[pl.ds(p * ys, ys)], 0, 1)
-        return carry
-
-    lax.fori_loop(0, planes, finish, 0)
-
     for copy in v_copies + e_copies + rs_copies + rg_copies + ag_copies + u_copies:
         copy.wait_send()
 
@@ -408,6 +421,18 @@
     def _():
         for copy in down:
             copy.wait_send()
+
+
+def finish_kernel(ret, out_hbm, stage, sem):
+    planes = out_hbm.shape[1]
+    ys = out_hbm.shape[2]
+    copies = []
+    for p in range(planes):
+        stage[p] = jnp.swapaxes(ret[p * ys : (p + 1) * ys], 0, 1)
+        copies.append(pltpu.make_async_copy(stage.at[p], out_hbm.at[:, p], sem.at[p]))
+        copies[-1].start()
+    for copy in copies:
+        copy.wait()
 
 
 def local(
@@ -427,12 +452,21 @@
     per = units // groups
     order = members * groups
     depth = order // slabs
-    terms, weight = scatter_terms(
-        groups, units, sensor_counts, sensor_offsets, observations, noise_scale, perturbation
-    )
+    slots = sensor_offsets.shape[0]
+    width = 2 * LANES
+    per_group = per * LANES // width
     vmem = pl.BlockSpec(memory_space=pltpu.VMEM)
     f32 = jnp.float32
     scratch = [
+        pltpu.VMEM((1, slots), jnp.int32),
+        pltpu.VMEM((1, slots), f32),
+        pltpu.VMEM((1, slots), f32),
+        pltpu.VMEM((members, slots), f32),
+        pltpu.VMEM((width, slots), jnp.bfloat16),
+        pltpu.VMEM((per_group * 2 * members, slots), jnp.bfloat16),
+        pltpu.VMEM((2 * members, slots), f32),
+        pltpu.VMEM((units, members, xsz), f32),
+        pltpu.VMEM((width // LANES, -(-per_group // 8) * 8, LANES), f32),
         pltpu.VMEM((members, planes + 4, ys, xsz), f32),
         pltpu.VMEM((3, planes + 2, ys, xsz), jnp.int32),
         pltpu.VMEM((planes + 2, ys, xsz), f32),
@@ -450,7 +484,7 @@
         pltpu.VMEM((depth, 2 * order), f32),
         pltpu.VMEM((order, 2 * order), f32),
         pltpu.VMEM((groups, per, members, xsz), f32),
-        pltpu.VMEM((units, members, xsz), f32),
+        pltpu.SemaphoreType.DMA((7,)),
         pltpu.SemaphoreType.DMA((2, 3)),
         pltpu.SemaphoreType.DMA((2, 3)),
         pltpu.SemaphoreType.DMA((4, groups)),
@@ -458,17 +492,38 @@
         pltpu.SemaphoreType.DMA((2, slabs)),
         pltpu.SemaphoreType.DMA((2, slabs)),
     ]
-    return pl.pallas_call(
+    anywhere = pl.BlockSpec(memory_space=pl.ANY)
+    ret = pl.pallas_call(
         functools.partial(step_kernel, groups, slabs),
-        out_shape=jax.ShapeDtypeStruct(fields.shape, f32),
-        in_specs=[vmem] * 5,
+        out_shape=jax.ShapeDtypeStruct((units, members, xsz), f32),
+        in_specs=[pl.BlockSpec(memory_space=pltpu.SMEM)] + [anywhere] * 7,
         out_specs=vmem,
         scratch_shapes=scratch,
         compiler_params=pltpu.CompilerParams(
             collective_id=0, has_side_effects=True, vmem_limit_bytes=56 * 1024 * 1024
         ),
         name="ensemble_step",
-    )(terms, weight, fields, velocity, diffusivity)
+    )(
+        sensor_counts,
+        sensor_offsets[None],
+        observations[None],
+        noise_scale[None],
+        perturbation,
+        fields,
+        velocity,
+        diffusivity,
+    )
+    return pl.pallas_call(
+        finish_kernel,
+        out_shape=jax.ShapeDtypeStruct(fields.shape, f32),
+        in_specs=[vmem],
+        out_specs=anywhere,
+        scratch_shapes=[
+            pltpu.VMEM((planes, members, ys, xsz), f32),
+            pltpu.SemaphoreType.DMA((planes,)),
+        ],
+        name="finish",
+    )(ret)
 
 
 def solution(mesh):

time: 60.1 us -> 48.5 us (0.81)
  local copies, waits for them, and re-layouts: 6.51 us -> 0 us
  Pallas kernels: 52.5 us -> 47.6 us
    unnamed x13 -> x0, local copies, waits for them, and re-layouts: 6.51 us -> none
    pallas_call x1, Pallas kernels: 8 us -> 1.9 us  [local(): pl.pallas_call(finish_kernel, out_shape=jax.ShapeDtypeStruct(fields.shape...]
    pallas_call x1, Pallas kernels: 44.5 us -> 45.7 us  [local(): pl.pallas_call(functools.partial(step_kernel, groups, slabs), out_shape=j...]
where the time goes in v2:
time: 48.5 us; the launch traced here: 48.3 us
  Pallas kernels  47.6 us (98%)
  between operations  0.66 us (1%)
    pallas_call x1, Pallas kernels, local(): pl.pallas_call(functools.partial(step_kernel, groups, slabs), out_shape=j...  45.7 us
    pallas_call x1, Pallas kernels, local(): pl.pallas_call(finish_kernel, out_shape=jax.ShapeDtypeStruct(fields.shape...  1.9 us

profile of v2, /device:TPU:0, one launch (start us, length us, event | category | flops | bytes accessed | tf_op | source)
XLA Modules:
  0.0 48.3 jit_solution(17576832891430812414)
XLA Ops:
  0.7 45.7 %ensemble_step.1.ret = f32[64,16,128]{2,1,0:T(8,128)} custom-call(s32[1]{0:T(128)S(6)} %copy.9.count_ref, s32[1,6144]{1,0:T(1,128)} %bitcast.3, f32[1,6144]{1,0:T(1,128)} %bitcast.4, f32[1,6144]{1,0:T(1,128)} %bitcast.5, f32[16,6144]{1,0:T(8,128)} %pert_hbm.1, f32[16,8,8,128]{3,2,1,0:T(8,128)} %fields_ref.1, s32[3,8,8,128]{3,2,1,0:T(8,128)} %vel_ref.1, ...), custom_call_target="tpu_custom_call" | custom-call | tf_op jit(solution)/shard_map/ensemble_step/pallas_call | solution.py:496
  46.4 1.9 %finish.1 = f32[16,8,8,128]{3,2,1,0:T(8,128)} custom-call(f32[64,16,128]{2,1,0:T(8,128)} %ensemble_step.1.ret), custom_call_target="tpu_custom_call" | custom-call | tf_op jit(solution)/shard_map/finish/pallas_call | solution.py:516

commit v3 on v2

--- a/solution.py
+++ b/solution.py
@@ -9,7 +9,7 @@
 
 STEPS = 2
 COURANT = 0.12
-EARLY = 3
+EARLY = 2
 LANES = 128
 BLOCK = 8
 MESH = pl.DeviceIdType.MESH
@@ -148,13 +148,15 @@
     gr_sem,
     ss_sem,
     sr_sem,
+    zs_sem,
+    zr_sem,
 ):
     g, s = lax.axis_index("grp"), lax.axis_index("slab")
     members, planes, ys, xsz = fields_ref.shape
     units = planes * ys
     per = units // groups
     order = members * groups
-    depth = order // slabs
+    depth = order // (2 * groups)
     last = planes + STEPS
 
     loads = [
@@ -174,18 +176,42 @@
     for copy in loads:
         copy.start()
 
+    core, z = lax.rem(s, 2), lax.div(s, 2)
+    place, places, heights = g * 2 + core, 2 * groups, slabs // 2
+
+    def plane_peer(r):
+        other = lax.rem(place + r, places)
+        return other, (lax.div(other, 2), z * 2 + lax.rem(other, 2))
+
+    def height_peer(r):
+        return (g, lax.rem(z + r, heights) * 2 + core)
+
     barrier = pltpu.get_barrier_semaphore()
-    for r in range(1, groups):
-        pl.semaphore_signal(
-            barrier, inc=1, device_id=(lax.rem(g + r, groups), s), device_id_type=MESH
-        )
-    for r in range(1, slabs):
-        pl.semaphore_signal(
-            barrier, inc=1, device_id=(g, lax.rem(s + r, slabs)), device_id_type=MESH
-        )
-    loads[0].wait()
-    spread_low(bt, off_ref[...])
-    pl.semaphore_wait(barrier, groups + slabs - 2)
+    for r in range(1, places):
+        pl.semaphore_signal(barrier, inc=1, device_id=plane_peer(r)[1], device_id_type=MESH)
+    for r in range(1, heights):
+        pl.semaphore_signal(barrier, inc=1, device_id=height_peer(r), device_id_type=MESH)
+    across = (g, lax.rem(s + 2 * core - 1 + slabs, slabs))
+    pl.semaphore_signal(barrier, inc=1, device_id=across, device_id_type=MESH)
+
+    def coefficients(p):
+        courant = [velx[c, p].astype(jnp.float32)[None] * COURANT for c in range(3)]
+        return courant + [difx[p][None]]
+
+    def first_step(p, carry):
+        mid[:, p] = advance(ext[:, p], ext[:, p + 1], ext[:, p + 2], *coefficients(p))
+        return carry
+
+    def second_step(p, carry):
+        res = advance(mid[:, p], mid[:, p + 1], mid[:, p + 2], *coefficients(p + 1))
+        own[pl.ds(p * ys, ys)] = jnp.swapaxes(res, 0, 1)
+        return carry
+
+    for copy in loads[4:]:
+        copy.wait()
+    lax.fori_loop(2, planes, first_step, 0)
+    lax.fori_loop(2, planes - 2, second_step, 0)
+    pl.semaphore_wait(barrier, places + heights - 1)
 
     def halo(sign, k, src, dst):
         return pltpu.make_async_remote_copy(
@@ -228,19 +254,39 @@
             device_id_type=MESH,
         )
 
-    def slab_copy(phase, r, src, dst):
+    def plane_copy(phase, r, src, dst):
         return pltpu.make_async_remote_copy(
             src_ref=src,
             dst_ref=dst,
             send_sem=ss_sem.at[phase, r],
             recv_sem=sr_sem.at[phase, r],
-            device_id=(g, lax.rem(s + r, slabs)),
+            device_id=plane_peer(r)[1],
             device_id_type=MESH,
         )
 
+    def height_copy(r, src, dst):
+        return pltpu.make_async_remote_copy(
+            src_ref=src,
+            dst_ref=dst,
+            send_sem=zs_sem.at[r],
+            recv_sem=zr_sem.at[r],
+            device_id=height_peer(r),
+            device_id_type=MESH,
+        )
+
     def units_of(r):
         return pl.ds(lax.rem(g + r, groups) * per, per)
 
+    def inner(r):
+        q = lax.rem(g + r, groups)
+        return jnp.logical_and(q * per >= 2 * ys, (q + 1) * per <= (planes - 2) * ys)
+
+    e_copies = [grp_copy(1, r, own.at[units_of(r)], eq.at[g]) for r in range(1, groups)]
+    for r, copy in enumerate(e_copies):
+        pl.when(inner(r + 1))(copy.start)
+
+    loads[0].wait()
+    spread_low(bt, off_ref[...])
     for copy in loads[1:4]:
         copy.wait()
     noise = noise_ref[...]
@@ -270,9 +316,6 @@
 
     lax.fori_loop(1, EARLY, scatter_turn, 0)
 
-    for copy in loads[4:]:
-        copy.wait()
-
     @pl.when(s == 0)
     def _():
         ext[:, 0:2] = jnp.zeros((members, 2, ys, xsz), jnp.float32)
@@ -295,15 +338,8 @@
         for copy in down:
             copy.wait_recv()
 
-    def coefficients(p):
-        courant = [velx[c, p].astype(jnp.float32)[None] * COURANT for c in range(3)]
-        return courant + [difx[p][None]]
-
-    def first_step(p, carry):
-        mid[:, p] = advance(ext[:, p], ext[:, p + 1], ext[:, p + 2], *coefficients(p))
-        return carry
-
-    lax.fori_loop(0, planes + 2, first_step, 0)
+    lax.fori_loop(0, 2, first_step, 0)
+    lax.fori_loop(planes, planes + 2, first_step, 0)
 
     @pl.when(s == 0)
     def _():
@@ -313,16 +349,10 @@
     def _():
         mid[:, planes + 1] = jnp.zeros((members, ys, xsz), jnp.float32)
 
-    def second_step(p, carry):
-        res = advance(mid[:, p], mid[:, p + 1], mid[:, p + 2], *coefficients(p + 1))
-        own[pl.ds(p * ys, ys)] = jnp.swapaxes(res, 0, 1)
-        return carry
-
-    lax.fori_loop(0, planes, second_step, 0)
-
-    e_copies = [grp_copy(1, r, own.at[units_of(r)], eq.at[g]) for r in range(1, groups)]
-    for copy in e_copies:
-        copy.start()
+    lax.fori_loop(0, 2, second_step, 0)
+    lax.fori_loop(planes - 2, planes, second_step, 0)
+    for r, copy in enumerate(e_copies):
+        pl.when(jnp.logical_not(inner(r + 1)))(copy.start)
     eq[g] = own[units_of(0)]
     lax.fori_loop(EARLY, groups + 1, scatter_turn, 0)
     vq[g] = v_ref[units_of(0)]
@@ -341,44 +371,49 @@
         w = w_ref[u % per_row, u // per_row : u // per_row + 1, :]
         centered = x - jnp.sum(x, axis=0, keepdims=True) / order
         xs[:, lanes] = x
-        xc[:, lanes] = centered
-        yz[0:order, lanes] = centered * w
-        yz[order : 2 * order, lanes] = v - x * w
+        first, second = split_two(centered)
+        high, low = split_two(jnp.concatenate([centered * w, v - x * w], axis=0))
+        for t, (left, right) in enumerate(((first, high), (first, low), (second, high))):
+            at = (t * per + u) * LANES
+            xc[:, at : at + LANES] = left.astype(jnp.bfloat16)
+            yz[:, at : at + LANES] = right.astype(jnp.bfloat16)
     part[...] = lax.dot_general(
         xc[...],
         yz[...],
         NT,
-        precision=lax.Precision.HIGHEST,
         preferred_element_type=jnp.float32,
     ) / (order - 1)
 
-    def rows_of(r):
-        return pl.ds(pl.multiple_of(lax.rem(s + r, slabs) * depth, depth), depth)
-
-    rs_copies = [slab_copy(0, r, part.at[rows_of(r)], rs.at[s]) for r in range(1, slabs)]
+    def rows_of(block):
+        return pl.ds(pl.multiple_of(block * depth, depth), depth)
+
+    rs_copies = [
+        plane_copy(0, r, part.at[rows_of(plane_peer(r)[0])], rs.at[place])
+        for r in range(1, places)
+    ]
     for copy in rs_copies:
         copy.start()
-    rs[s] = part[rows_of(0), :]
+    rs[place] = part[rows_of(place), :]
     for copy in rs_copies:
         copy.wait_recv()
     added = rs[0]
-    for i in range(1, slabs):
+    for i in range(1, places):
         added = added + rs[i]
     rowsum[...] = added
-    rg_copies = [grp_copy(2, r, rowsum, rg.at[g]) for r in range(1, groups)]
+    rg_copies = [height_copy(r, rowsum, rg.at[z]) for r in range(1, heights)]
     for copy in rg_copies:
         copy.start()
-    rg[g] = added
+    rg[z] = added
     for copy in rg_copies:
         copy.wait_recv()
     added = rg[0]
-    for i in range(1, groups):
+    for i in range(1, heights):
         added = added + rg[i]
     total[...] = added
-    ag_copies = [slab_copy(1, r, total, m_ref.at[rows_of(0)]) for r in range(1, slabs)]
+    ag_copies = [plane_copy(1, r, total, m_ref.at[rows_of(place)]) for r in range(1, places)]
     for copy in ag_copies:
         copy.start()
-    m_ref[rows_of(0), :] = added
+    m_ref[rows_of(place), :] = added
     for copy in ag_copies:
         copy.wait_recv()
 
@@ -400,7 +435,7 @@
         for u in range(per):
             upd[q, u] = new[q * members : (q + 1) * members, u * LANES : (u + 1) * LANES]
     u_copies = [
-        grp_copy(3, r, upd.at[lax.rem(g + r, groups)], ret.at[units_of(0)])
+        grp_copy(2, r, upd.at[lax.rem(g + r, groups)], ret.at[units_of(0)])
         for r in range(1, groups)
     ]
     for copy in u_copies:
@@ -451,7 +486,7 @@
     units = planes * ys
     per = units // groups
     order = members * groups
-    depth = order // slabs
+    depth = order // (2 * groups)
     slots = sensor_offsets.shape[0]
     width = 2 * LANES
     per_group = per * LANES // width
@@ -475,22 +510,24 @@
         pltpu.VMEM((groups, per, members, xsz), f32),
         pltpu.VMEM((groups, per, members, xsz), f32),
         pltpu.VMEM((order, per * xsz), f32),
-        pltpu.VMEM((order, per * xsz), f32),
-        pltpu.VMEM((2 * order, per * xsz), f32),
+        pltpu.VMEM((order, 3 * per * xsz), jnp.bfloat16),
+        pltpu.VMEM((2 * order, 3 * per * xsz), jnp.bfloat16),
         pltpu.VMEM((order, 2 * order), f32),
-        pltpu.VMEM((slabs, depth, 2 * order), f32),
+        pltpu.VMEM((2 * groups, depth, 2 * order), f32),
         pltpu.VMEM((depth, 2 * order), f32),
-        pltpu.VMEM((groups, depth, 2 * order), f32),
+        pltpu.VMEM((slabs // 2, depth, 2 * order), f32),
         pltpu.VMEM((depth, 2 * order), f32),
         pltpu.VMEM((order, 2 * order), f32),
         pltpu.VMEM((groups, per, members, xsz), f32),
         pltpu.SemaphoreType.DMA((7,)),
         pltpu.SemaphoreType.DMA((2, 3)),
         pltpu.SemaphoreType.DMA((2, 3)),
-        pltpu.SemaphoreType.DMA((4, groups)),
-        pltpu.SemaphoreType.DMA((4, groups)),
-        pltpu.SemaphoreType.DMA((2, slabs)),
-        pltpu.SemaphoreType.DMA((2, slabs)),
+        pltpu.SemaphoreType.DMA((3, groups)),
+        pltpu.SemaphoreType.DMA((3, groups)),
+        pltpu.SemaphoreType.DMA((2, 2 * groups)),
+        pltpu.SemaphoreType.DMA((2, 2 * groups)),
+        pltpu.SemaphoreType.DMA((slabs // 2,)),
+        pltpu.SemaphoreType.DMA((slabs // 2,)),
     ]
     anywhere = pl.BlockSpec(memory_space=pl.ANY)
     ret = pl.pallas_call(

time: 48.5 us -> 47.9 us (0.988)
  Pallas kernels: 47.6 us -> 47.1 us
    pallas_call x1, Pallas kernels: 45.7 us -> 45.2 us  [local(): pl.pallas_call(functools.partial(step_kernel, groups, slabs), out_shape=j...]
where the time goes in v3:
time: 47.9 us; the launch traced here: 47.8 us
  Pallas kernels  47.1 us (98%)
  between operations  0.66 us (1%)
    pallas_call x1, Pallas kernels, local(): pl.pallas_call(functools.partial(step_kernel, groups, slabs), out_shape=j...  45.2 us
    pallas_call x1, Pallas kernels, local(): pl.pallas_call(finish_kernel, out_shape=jax.ShapeDtypeStruct(fields.shape...  1.9 us

profile of v3, /device:TPU:0, one launch (start us, length us, event | category | flops | bytes accessed | tf_op | source)
XLA Modules:
  0.0 47.8 jit_solution(10208669061558239075)
XLA Ops:
  0.7 45.2 %ensemble_step.1.ret = f32[64,16,128]{2,1,0:T(8,128)} custom-call(s32[1]{0:T(128)S(6)} %copy.9.count_ref, s32[1,6144]{1,0:T(1,128)} %bitcast.3, f32[1,6144]{1,0:T(1,128)} %bitcast.4, f32[1,6144]{1,0:T(1,128)} %bitcast.5, f32[16,6144]{1,0:T(8,128)} %pert_hbm.1, f32[16,8,8,128]{3,2,1,0:T(8,128)} %fields_ref.1, s32[3,8,8,128]{3,2,1,0:T(8,128)} %vel_ref.1, ...), custom_call_target="tpu_custom_call" | custom-call | tf_op jit(solution)/shard_map/ensemble_step/pallas_call | solution.py:533
  45.8 1.9 %finish.1 = f32[16,8,8,128]{3,2,1,0:T(8,128)} custom-call(f32[64,16,128]{2,1,0:T(8,128)} %ensemble_step.1.ret), custom_call_target="tpu_custom_call" | custom-call | tf_op jit(solution)/shard_map/finish/pallas_call | solution.py:553
